TPU v7x, 32 devices: a whole 2x2x4 slice. The times are simulated.
32 devices in a mesh: img: 8 (over z, core), txt: 4 (over y, x).
Axes of the slice: x: 2, y: 2, z: 4, core: 2. Of those that a mesh axis runs over, the one named last changes fastest.
Arguments:
- image_emb: float32 [1024, 1536], P('img', 'txt'), may hold values from -0.15625 to 0.15625
- text_emb: float32 [1024, 1536], P('txt', 'img'), may hold values from -0.15625 to 0.15625
- vision_feat: bfloat16 [1024, 5120], P('img', 'txt'), may hold values from -0.125 to 0.125
- positive: int32 [1024], P('img'), may hold values from 0 to 1023, each once
- logit_scale: float32 [1], replicated, may hold values from 5 to 15
- logit_bias: float32 [1], replicated, may hold values from -3 to -1
Outputs:
- grad_image: float32 [1024, 1536], P('img', 'txt')
- grad_text: float32 [1024, 1536], P('txt', 'img')
- grad_proj: float32 [5120, 1536], P('txt', 'img')
Inputs may be any that keep to these rules, and one draw needn't show every extreme that they name: `positive`: each text index is the match of exactly one image.
All inputs are finite; a program needn't handle non-finite values.
Results may differ from a plain program's by a relative error of at most 0.0029.
Values may be sent and summed in bfloat16 or wider, within the bound.
A program may use at most 64 MiB of HBM per device.

v0:
```python
import jax
import jax.numpy as jnp
from jax import lax
from jax.sharding import PartitionSpec as P


def per_device(image_emb, text_emb, vision_feat, positive, logit_scale, logit_bias):
    scale = logit_scale[0]
    bias = logit_bias[0]
    image_full = lax.all_gather(image_emb, "txt", axis=1, tiled=True)
    text_full = lax.all_gather(text_emb, "img", axis=1, tiled=True)
    text_rows = text_full.shape[0]
    first_col = lax.axis_index("txt") * text_rows
    columns = first_col + lax.iota(jnp.int32, text_rows)
    logits = (
        scale
        * jnp.dot(
            image_full,
            text_full.T,
            precision=lax.Precision.HIGHEST,
            preferred_element_type=jnp.float32,
        )
        + bias
    )
    sign = jnp.where(positive[:, None] == columns[None, :], 1.0, -1.0).astype(jnp.float32)
    slope = -sign * jax.nn.sigmoid(-sign * logits)
    image_terms = scale * jnp.dot(
        slope, text_full, precision=lax.Precision.HIGHEST, preferred_element_type=jnp.float32
    )
    text_terms = scale * jnp.dot(
        slope.T, image_full, precision=lax.Precision.HIGHEST, preferred_element_type=jnp.float32
    )
    grad_text = lax.psum_scatter(text_terms, "img", scatter_dimension=1, tiled=True)
    grad_image = lax.psum_scatter(image_terms, "txt", scatter_dimension=1, tiled=True)
    image_low = lax.all_gather(grad_image.astype(jnp.bfloat16), "txt", axis=1, tiled=True)
    weight_terms = jnp.dot(vision_feat.T, image_low, preferred_element_type=jnp.float32)
    grad_proj = lax.psum_scatter(weight_terms, "img", scatter_dimension=1, tiled=True)
    return (grad_image, grad_text, grad_proj)


def solution(mesh):
    placed = (P("img", "txt"), P("txt", "img"), P("img", "txt"), P("img"), P(), P())
    return jax.shard_map(
        per_device,
        mesh=mesh,
        in_specs=placed,
        out_specs=(P("img", "txt"), P("txt", "img"), P("txt", "img")),
        check_vma=False,
    )
```

profile of v0, /device:TPU:0, one launch (start us, length us, event | category | flops | bytes accessed | tf_op | source)
XLA Modules:
  0.0 197.5 jit_solution(13368164841383276758)
XLA Ops:
  7.2 0.0 copy-start
  7.2 0.0 all-gather.2.cloned.1.call-start
  7.2 0.7 all-gather.2.cloned.1.call-update
  7.9 0.0 reduce-scatter.4.cloned.1.call-start
  9.3 15.9 %all_gather.9 = f32[128,1536]{1,0:T(8,128)S(1)} all-gather(f32[128,384]{1,0:T(8,128)} %param.6), channel_id=1, replica_groups=mesh['img'=8,'txt'=4] {'txt'}, dimensions={1}, use_global_device_ids=true | all-gather | bytes 983040 | tf_op jit(solution)/shard_map/all_gather | solution.py:10
  25.2 12.5 %all-gather.2.cloned.1.call-done = f32[256,1536]{0,1:T(8,128)} async-done(((f32[256,192]{0,1:T(8,128)}), f32[256,1536]{0,1:T(8,128)}) %all-gather.2.cloned.1.call-update) | async-done | bytes 1572880 | tf_op jit(solution)/shard_map/all_gather | solution.py:11
  37.7 0.0 copy-start.1
  37.7 2.4 %fusion.6 = f32[128,256]{1,0:T(8,128)S(1)} fusion(f32[128,1536]{1,0:T(8,128)S(1)} %all_gather.9, f32[256,1536]{0,1:T(8,128)} %all-gather.2.cloned.1.call-done, f32[]{:T(128)} %bitcast.15, f32[]{:T(128)} %bitcast.13, s32[256]{0:T(256)S(1)} %iota_add_fusion, s32[128]{0:T(128)} %param.9), kind=kOutput, calls=%fused_computation.10 | convolution fusion | flops 604307456 | bytes 2491912 | tf_op jit(solution)/shard_map/dot_general | solution.py:17
  40.1 0.0 copy-done.1
  40.1 2.6 %convolution_multiply_fusion.1 = f32[128,1536]{1,0:T(8,128)} fusion(f32[128,256]{1,0:T(8,128)S(1)} %fusion.6, f32[256,1536]{0,1:T(8,128)S(1)} %copy-done.1, f32[]{:T(128)} %bitcast.12), kind=kOutput, calls=%fused_computation.2 | convolution fusion | flops 604176384 | bytes 2490372 | tf_op jit(solution)/shard_map/dot_general | solution.py:27
  42.7 0.0 reduce-scatter.4.cloned.1.call-update
  42.7 0.0 reduce-scatter.6.cloned.1.call-start
  42.8 2.7 %convolution_multiply_fusion = f32[256,1536]{0,1:T(8,128)} fusion(f32[128,256]{1,0:T(8,128)S(1)} %fusion.6, f32[128,1536]{1,0:T(8,128)S(1)} %all_gather.9, f32[]{:T(128)} %bitcast.14), kind=kOutput, calls=%fused_computation.1 | convolution fusion | flops 604372992 | bytes 2490372 | tf_op jit(solution)/shard_map/dot_general | solution.py:30
  45.4 0.0 reduce-scatter.6.cloned.1.call-update
  45.5 0.0 reduce-scatter.8.cloned.1.call-start
  45.5 22.7 %reduce-scatter.4.cloned.1.call-done = f32[128,384]{1,0:T(8,128)} async-done(((f32[128,1536]{1,0:T(8,128)}), f32[128,384]{1,0:T(8,128)}) %reduce-scatter.4.cloned.1.call-update) | async-done | bytes 196624 | tf_op jit(solution)/shard_map/reduce_scatter | solution.py:34
  68.2 0.9 convert_element_type.3
  69.1 10.1 %all_gather.11 = bf16[128,1536]{1,0:T(8,128)(2,1)S(1)} all-gather(bf16[128,384]{1,0:T(8,128)(2,1)S(1)} %convert_element_type.3), channel_id=1, replica_groups=mesh['img'=8,'txt'=4] {'txt'}, dimensions={1}, use_global_device_ids=true | all-gather | bytes 491520 | tf_op jit(solution)/shard_map/all_gather | solution.py:35
  79.2 0.0 copy-done
  79.2 4.3 %convolution_bitcast_fusion = f32[1280,1536]{0,1:T(8,128)} fusion(bf16[128,1536]{1,0:T(8,128)(2,1)S(1)} %all_gather.11, bf16[128,1280]{1,0:T(8,128)(2,1)S(1)} %copy-done), kind=kOutput, calls=%fused_computation | convolution fusion | flops 503316480 | bytes 8585216 | tf_op jit(solution)/shard_map/dot_general | solution.py:36
  83.5 0.0 reduce-scatter.8.cloned.1.call-update
  83.5 21.9 %reduce-scatter.6.cloned.1.call-done = f32[256,192]{0,1:T(8,128)} async-done(((f32[256,1536]{0,1:T(8,128)}), f32[256,192]{0,1:T(8,128)}) %reduce-scatter.6.cloned.1.call-update) | async-done | bytes 196624 | tf_op jit(solution)/shard_map/reduce_scatter | solution.py:33
  105.4 85.6 %reduce-scatter.8.cloned.1.call-done = f32[1280,192]{0,1:T(8,128)} async-done(((f32[1280,1536]{0,1:T(8,128)}), f32[1280,192]{0,1:T(8,128)}) %reduce-scatter.8.cloned.1.call-update) | async-done | bytes 983056 | tf_op jit(solution)/shard_map/reduce_scatter | solution.py:37
  (1 shorter events, 0.0 us)
Async XLA Ops:
  7.2 72.1 %copy-start = (bf16[128,1280]{1,0:T(8,128)(2,1)S(1)}, bf16[128,1280]{1,0:T(8,128)(2,1)}, u32[]{:S(2)}) copy-start(bf16[128,1280]{1,0:T(8,128)(2,1)} %param.8) | copy-start | bytes 983044
  7.2 30.5 %all-gather.2.cloned.1.call-start = ((), (), s32[]{:S(2)}) async-start(), calls=%async_computation.3 | async-start | bytes 1769472 | tf_op jit(solution)/shard_map/all_gather | solution.py:11
  7.9 60.3 %reduce-scatter.4.cloned.1.call-start = ((), (), s32[]{:S(2)}) async-start(), calls=%async_computation.4 | async-start | bytes 983040 | tf_op jit(solution)/shard_map/reduce_scatter | solution.py:34
  37.7 2.5 %copy-start.1 = (f32[256,1536]{0,1:T(8,128)S(1)}, f32[256,1536]{0,1:T(8,128)}, u32[]{:S(2)}) copy-start(f32[256,1536]{0,1:T(8,128)} %all-gather.2.cloned.1.call-done) | copy-start | bytes 4718596
  42.7 62.7 %reduce-scatter.6.cloned.1.call-start = ((), (), s32[]{:S(2)}) async-start(), calls=%async_computation.5 | async-start | bytes 1769472 | tf_op jit(solution)/shard_map/reduce_scatter | solution.py:33
  45.5 145.5 %reduce-scatter.8.cloned.1.call-start = ((), (), s32[]{:S(2)}) async-start(), calls=%async_computation.6 | async-start | bytes 8847360 | tf_op jit(solution)/shard_map/reduce_scatter | solution.py:37
Sparse Core Ops, SparseCore 0:
  9.6 27.9 all-gather.1
  42.9 25.2 reduce-scatter.3
  71.1 34.2 reduce-scatter.5
  108.1 82.8 reduce-scatter.7
where the time goes:
time: 198 us
  waiting for transfers between devices  143 us (72%)
  blocking collectives  26 us (13%)
  between operations  15.1 us (8%)
  matrix products  12 us (6%)
    reduce_scatter x1, waiting for transfers between devices, per_device(): lax.psum_scatter(weight_terms, 'img', scatter_dimension=1, tiled=True)  85.6 us
    reduce_scatter x1, waiting for transfers between devices, per_device(): lax.psum_scatter(image_terms, 'txt', scatter_dimension=1, tiled=True)  22.7 us
    reduce_scatter x1, waiting for transfers between devices, per_device(): lax.psum_scatter(text_terms, 'img', scatter_dimension=1, tiled=True)  21.9 us
    all_gather x1, blocking collectives, per_device(): image_full = lax.all_gather(image_emb, 'txt', axis=1, tiled=True)  15.9 us
    all_gather x1, waiting for transfers between devices, per_device(): text_full = lax.all_gather(text_emb, 'img', axis=1, tiled=True)  12.5 us
    all_gather x1, blocking collectives, per_device(): lax.all_gather(grad_image.astype(jnp.bfloat16), 'txt', axis=1, tiled=True)  10.1 us
    dot_general x1, matrix products, per_device(): jnp.dot(vision_feat.T, image_low, preferred_element_type=jnp.float32)  4.28 us
  transfers between devices with their start and end apart: 4, of which 4 were waited for; matrix products, arithmetic and copies ran while one was open for 4% of the time, Pallas kernels for 0%

commit v1 on v0

v1 whole, which is shorter than its diff:
```python
import functools

import jax
import jax.numpy as jnp
from jax import lax
from jax.experimental import pallas as pl
from jax.experimental.pallas import tpu as pltpu
from jax.sharding import PartitionSpec as P

MESH = pl.DeviceIdType.MESH
F32 = jnp.float32
BF16 = jnp.bfloat16


def kernel(
    n_img, n_txt,
    scale_ref, bias_ref, pos_ref, img_ref, txt_ref, vis_ref,
    gi_ref, gt_ref, gp_ref,
    img_full, txt_full, vis_full, pimg, rs_img, gsend, grecv, low_send, low_recv,
    ptxt, txt_pair, txt_low, rs_txt,
    i_s, i_r, t_s, t_r, tp_s, tp_r, v_s, v_r, vp_s, vp_r, a_s, a_r, g_s, g_r,
    l_s, l_r, m_s, m_r, x_s, x_r, r_s, r_r,
):
    pairs = n_img // 2
    me_i = lax.axis_index("img")
    me_t = lax.axis_index("txt")
    p = me_i // 2
    c = lax.rem(me_i, 2)
    mate = 2 * p + 1 - c
    et = img_ref.shape[0]
    ei = txt_ref.shape[0]
    rows = img_ref.shape[1]
    cols = txt_ref.shape[1]
    part = rows // n_txt

    def img_of(k):
        return lax.rem(me_i + k, n_img)

    def txt_of(k):
        return lax.rem(me_t + k, n_txt)

    def pair_of(k):
        return lax.rem(p + k + pairs, pairs)

    def remote(src, dst, ss, rs, i, t):
        return pltpu.make_async_remote_copy(
            src_ref=src, dst_ref=dst, send_sem=ss, recv_sem=rs,
            device_id=(i, t), device_id_type=MESH,
        )

    def txt_rows(i):
        return pl.ds(pl.multiple_of(i * ei, ei), ei)

    def img_rows(t):
        return pl.ds(pl.multiple_of(t * et, et), et)

    def vis_rows(i):
        return pl.ds(pl.multiple_of(i * rows, rows), rows)

    barrier = pltpu.get_barrier_semaphore()
    for k in range(1, n_img):
        pl.semaphore_signal(barrier, inc=1, device_id=(img_of(k), me_t), device_id_type=MESH)
    for k in range(1, n_txt):
        pl.semaphore_signal(barrier, inc=1, device_id=(me_i, txt_of(k)), device_id_type=MESH)
    pl.semaphore_wait(barrier, n_img + n_txt - 2)

    mine_t = txt_full.at[txt_rows(me_i), :]
    text_z = [
        remote(txt_ref, mine_t, t_s.at[k - 1], t_r.at[k - 1], 2 * pair_of(k) + c, me_t)
        for k in range(1, pairs)
    ]
    text_mate = [remote(txt_ref, mine_t, tp_s.at[0], tp_r.at[0], mate, me_t)]
    image_x = [
        remote(img_ref, img_full.at[img_rows(me_t), :], i_s.at[k - 1], i_r.at[k - 1], me_i, txt_of(k))
        for k in range(1, n_txt)
    ]
    for copy in text_z + text_mate + image_x:
        copy.start()
    vis_ring = []
    vis_mate = []

    def send_vis(step):
        block = vis_rows(2 * pair_of(-step) + c)
        src = vis_ref if step == 0 else vis_full.at[block, :]
        if step < pairs - 1:
            ring = remote(src, vis_full.at[block, :], v_s.at[step], v_r.at[step], 2 * pair_of(1) + c, me_t)
            ring.start()
            vis_ring.append(ring)
        pair = remote(src, vis_full.at[block, :], vp_s.at[step], vp_r.at[step], mate, me_t)
        pair.start()
        vis_mate.append(pair)

    send_vis(0)
    txt_full[txt_rows(me_i), :] = txt_ref[...]
    img_full[img_rows(me_t), :] = img_ref[...]
    vis_full[vis_rows(me_i), :] = vis_ref[...]
    for k in range(1, pairs):
        text_z[k - 1].wait_recv()
        block = txt_full.at[txt_rows(2 * pair_of(-k) + c), :]
        copy = remote(block, block, tp_s.at[k], tp_r.at[k], mate, me_t)
        copy.start()
        text_mate.append(copy)
    for copy in image_x + text_mate:
        copy.wait_recv()

    scale = scale_ref[0]
    bias = bias_ref[0]
    image = img_full[...]
    text = txt_full[...]
    logits = scale * lax.dot_general(
        image, text, (((0,), (0,)), ((), ())), preferred_element_type=F32
    ) + bias
    column = me_t * cols + lax.broadcasted_iota(jnp.int32, (rows, cols), 1)
    sign = jnp.where(pos_ref[...] == column, 1.0, -1.0).astype(F32)
    slope = -sign / (1.0 + jnp.exp(sign * logits))
    high = slope.astype(BF16)
    rest = (slope - high.astype(F32)).astype(BF16)

    nt = (((1,), (1,)), ((), ()))
    pimg[...] = lax.dot_general(high, text, nt, preferred_element_type=F32) + lax.dot_general(
        rest, text, nt, preferred_element_type=F32
    )

    def part_rows(t):
        return pl.ds(pl.multiple_of(t * part, part), part)

    image_rs = [
        remote(pimg.at[part_rows(txt_of(k)), :], rs_img.at[k - 1], a_s.at[k - 1], a_r.at[k - 1], me_i, txt_of(k))
        for k in range(1, n_txt)
    ]
    for copy in image_rs:
        copy.start()

    ptxt[...] = jnp.dot(image, high, preferred_element_type=F32) + jnp.dot(
        image, rest, preferred_element_type=F32
    )
    text_pair = [
        remote(ptxt.at[txt_rows(2 * q + 1 - c), :], txt_pair.at[q], x_s.at[q], x_r.at[q], mate, me_t)
        for q in range(pairs)
    ]
    for copy in text_pair:
        copy.start()

    def step_vis(step):
        vis_ring[step - 1].wait_recv()
        send_vis(step)

    for step in range(1, pairs - 1):
        step_vis(step)

    for copy in image_rs:
        copy.wait_recv()
    total = pimg[part_rows(me_t), :]
    for k in range(n_txt - 1):
        total = total + rs_img[k]
    total = scale * total
    low = total.astype(BF16)
    for i in range(n_img):
        low_send[i] = low[:, i * ei:(i + 1) * ei]
    low_z = [
        remote(low_send.at[img_of(k)], low_recv.at[me_i, me_t], l_s.at[k - 1], l_r.at[k - 1], img_of(k), me_t)
        for k in range(1, n_img)
    ]
    for copy in low_z:
        copy.start()
    for t in range(n_txt):
        gsend[t] = total[:, t * et:(t + 1) * et]
    grad_x = [
        remote(gsend.at[txt_of(k)], grecv.at[me_t], g_s.at[k - 1], g_r.at[k - 1], me_i, txt_of(k))
        for k in range(1, n_txt)
    ]
    low_recv[me_i, me_t] = low_send[me_i]
    for copy in low_z:
        copy.wait_recv()
    low_x = [
        remote(low_recv.at[:, me_t], low_recv.at[:, me_t], m_s.at[k - 1], m_r.at[k - 1], me_i, txt_of(k))
        for k in range(1, n_txt)
    ]
    for copy in low_x + grad_x:
        copy.start()

    step_vis(pairs - 1)

    for q in range(pairs):
        text_pair[q].wait_recv()
        txt_pair[q] = txt_pair[q] + ptxt[txt_rows(2 * q + c), :]
        txt_low[q] = txt_pair[q].astype(BF16)
    text_rs = [
        remote(txt_low.at[pair_of(k)], rs_txt.at[k - 1], r_s.at[k - 1], r_r.at[k - 1], 2 * pair_of(k) + c, me_t)
        for k in range(1, pairs)
    ]
    for copy in text_rs:
        copy.start()

    for copy in low_x + vis_mate:
        copy.wait_recv()
    if part % 16:
        low_all = low_recv[...].astype(F32).reshape(n_img * rows, ei).astype(BF16)
    else:
        low_all = low_recv[...].reshape(n_img * rows, ei)
    gp_ref[...] = lax.dot_general(
        low_all, vis_full[...], (((0,), (0,)), ((), ())), preferred_element_type=F32
    )

    for copy in grad_x:
        copy.wait_recv()
    gi_ref[...] = grecv[...]
    gi_ref[me_t] = gsend[me_t]
    for copy in text_rs:
        copy.wait_recv()
    total = txt_pair[p]
    for k in range(pairs - 1):
        total = total + rs_txt[k].astype(F32)
    gt_ref[...] = scale * total
    for copy in text_z + text_mate + image_x + vis_ring + vis_mate + image_rs + text_pair + low_z + low_x + grad_x + text_rs:
        copy.wait_send()


def per_device(n_img, n_txt, image_emb, text_emb, vision_feat, positive, logit_scale, logit_bias):
    image = image_emb.T.astype(BF16)
    text = text_emb.T.astype(BF16)
    et, rows = image.shape
    ei, cols = text.shape
    emb = et * n_txt
    vis = vision_feat.shape[1]
    part = rows // n_txt
    pairs = n_img // 2
    dma = lambda n: pltpu.SemaphoreType.DMA((n,))
    vmem = pl.BlockSpec(memory_space=pltpu.VMEM)
    smem = pl.BlockSpec(memory_space=pltpu.SMEM)
    gi, gt, gp = pl.pallas_call(
        functools.partial(kernel, n_img, n_txt),
        out_shape=(
            jax.ShapeDtypeStruct((n_txt, part, et), F32),
            jax.ShapeDtypeStruct((ei, cols), F32),
            jax.ShapeDtypeStruct((ei, vis), F32),
        ),
        in_specs=[smem, smem, vmem, vmem, vmem, vmem],
        out_specs=(vmem, vmem, vmem),
        scratch_shapes=[
            pltpu.VMEM((emb, rows), BF16),
            pltpu.VMEM((emb, cols), BF16),
            pltpu.VMEM((n_img * rows, vis), BF16),
            pltpu.VMEM((rows, emb), F32),
            pltpu.VMEM((n_txt - 1, part, emb), F32),
            pltpu.VMEM((n_txt, part, et), F32),
            pltpu.VMEM((n_txt, part, et), F32),
            pltpu.VMEM((n_img, part, ei), BF16),
            pltpu.VMEM((n_img, n_txt, part, ei), BF16),
            pltpu.VMEM((emb, cols), F32),
            pltpu.VMEM((pairs, ei, cols), F32),
            pltpu.VMEM((pairs, ei, cols), BF16),
            pltpu.VMEM((pairs - 1, ei, cols), BF16),
            dma(n_txt - 1), dma(n_txt - 1),
            dma(pairs - 1), dma(pairs - 1), dma(pairs), dma(pairs),
            dma(pairs - 1), dma(pairs - 1), dma(pairs), dma(pairs),
            dma(n_txt - 1), dma(n_txt - 1), dma(n_txt - 1), dma(n_txt - 1),
            dma(n_img - 1), dma(n_img - 1), dma(n_txt - 1), dma(n_txt - 1),
            dma(pairs), dma(pairs), dma(pairs - 1), dma(pairs - 1),
        ],
        compiler_params=pltpu.CompilerParams(
            collective_id=0, has_side_effects=True, vmem_limit_bytes=60 * 1024 * 1024
        ),
    )(logit_scale, logit_bias, positive.reshape(rows, 1), image, text, vision_feat)
    return gi.reshape(rows, et), gt.T, gp.T


def solution(mesh):
    placed = (P("img", "txt"), P("txt", "img"), P("img", "txt"), P("img"), P(), P())
    return jax.shard_map(
        functools.partial(per_device, mesh.shape["img"], mesh.shape["txt"]),
        mesh=mesh,
        in_specs=placed,
        out_specs=(P("img", "txt"), P("txt", "img"), P("txt", "img")),
        check_vma=False,
    )
```

time: 198 us -> 76.7 us (0.39)
  waiting for transfers between devices: 143 us -> 0 us
  Pallas kernels: 0 us -> 66.2 us
  blocking collectives: 26 us -> 0 us
  between operations: 15.1 us -> 1.99 us
  matrix products: 12 us -> 0 us
  local copies, waits for them, and re-layouts: 0.01 us -> 7.61 us
    reduce_scatter x3 -> x0, waiting for transfers between devices: 130 us -> none  [the longest x1 85.6 us: per_device(): lax.psum_scatter(weight_terms, 'img', scatter_dimension=1, tiled=True)]
    pallas_call x0 -> x1, Pallas kernels: none -> 66.2 us  [per_device(): pl.pallas_call(functools.partial(kernel, n_img, n_txt), out_shape=(jax.Sh...]
    all_gather x2 -> x0, blocking collectives: 26 us -> none  [the longest x1 15.9 us: per_device(): image_full = lax.all_gather(image_emb, 'txt', axis=1, tiled=True)]
    all_gather x1 -> x0, waiting for transfers between devices: 12.5 us -> none  [per_device(): text_full = lax.all_gather(text_emb, 'img', axis=1, tiled=True)]
    dot_general x4 -> x0, matrix products: 12 us -> none  [the longest x1 4.28 us: per_device(): jnp.dot(vision_feat.T, image_low, preferred_element_type=jnp.float32)]
    unnamed x4 -> x8, local copies, waits for them, and re-layouts: 0.01 us -> 6.22 us
  transfers between devices with their start and end apart: 4 -> 0, of which waited for: 4 -> 0; matrix products, arithmetic and copies ran while one was open for 4% -> 0% of each run, Pallas kernels for 0% -> 0%
where the time goes in v1:
time: 76.7 us; the launch traced here: 76.4 us
  Pallas kernels  66.2 us (86%)
  local copies, waits for them, and re-layouts  7.61 us (10%)
  between operations  1.99 us (3%)
    pallas_call x1, Pallas kernels, per_device(): pl.pallas_call(functools.partial(kernel, n_img, n_txt), out_shape=(jax.Sh...  66.2 us
    unnamed x8, local copies, waits for them, and re-layouts  6.22 us

profile of v1, /device:TPU:0, one launch (start us, length us, event | category | flops | bytes accessed | tf_op | source)
XLA Modules:
  0.0 76.4 jit_solution(9561337058863956124)
XLA Ops:
  0.6 0.0 copy-start
  2.0 1.4 %copy.10.pos_ref = s32[128,1]{1,0:T(8,128)} copy(s32[128,1]{0,1:T(1,128)} %bitcast.13) | data formatting | bytes 1024 | tf_op jit(solution)/shard_map/reshape | solution.py:264
  3.4 1.7 %copy.9 = bf16[128,384]{0,1:T(8,128)(2,1)} copy(f32[128,384]{1,0:T(8,128)} %param.6) | data formatting | bytes 294912 | tf_op args[0]
  5.0 0.0 copy-done
  5.0 0.7 convert_bitcast_fusion.txt_ref
  5.7 66.2 %shard_map.85 = (f32[4,32,384]{2,1,0:T(8,128)}, f32[192,256]{1,0:T(8,128)}, f32[192,1280]{1,0:T(8,128)}) custom-call(f32[1]{0:T(128)S(6)} %copy.14.scale_ref, f32[1]{0:T(128)S(6)} %copy.15.bias_ref, s32[128,1]{1,0:T(8,128)} %copy.10.pos_ref, bf16[384,128]{1,0:T(8,128)(2,1)} %bitcast.10, bf16[192,256]{1,0:T(8,128)(2,1)} %convert_bitcast_fusion.txt_ref, ...), custom_call_target="tpu_custom_call" | custom-call | tf_op jit(solution)/shard_map/pallas_call | solution.py:231
  71.9 0.0 copy-start.1
  71.9 1.7 %copy.16 = f32[128,384]{1,0:T(8,128)} copy(f32[128,384]{1,0:T(8,128)} %bitcast.12) | data formatting | bytes 393216
  73.5 0.0 copy-done.1
  73.6 0.7 copy.17
  74.2 2.2 %copy.18 = f32[1280,192]{0,1:T(8,128)} copy(f32[1280,192]{0,1:T(8,128)} %bitcast.9) | data formatting | bytes 1966080
Async XLA Ops:
  0.6 4.4 %copy-start = (f32[256,192]{0,1:T(8,128)S(1)}, f32[256,192]{0,1:T(8,128)}, u32[]{:S(2)}) copy-start(f32[256,192]{0,1:T(8,128)} %param.7) | copy-start | bytes 589828
  71.9 1.7 %copy-start.1 = (f32[192,256]{1,0:T(8,128)S(1)}, f32[192,256]{1,0:T(8,128)}, u32[]{:S(2)}) copy-start(f32[192,256]{1,0:T(8,128)} %get-tuple-element.7) | copy-start | bytes 589828

commit v2 on v1

--- a/solution.py
+++ b/solution.py
@@ -16,9 +16,9 @@
     n_img, n_txt,
     scale_ref, bias_ref, pos_ref, img_ref, txt_ref, vis_ref,
     gi_ref, gt_ref, gp_ref,
-    img_full, txt_full, vis_full, pimg, rs_img, gsend, grecv, low_send, low_recv,
+    img_full, txt_full, txt_rest, vis_full, pimg, rs_img, gsend, grecv, low_send, low_recv,
     ptxt, txt_pair, txt_low, rs_txt,
-    i_s, i_r, t_s, t_r, tp_s, tp_r, v_s, v_r, vp_s, vp_r, a_s, a_r, g_s, g_r,
+    i_s, i_r, t_s, t_r, tp_s, tp_r, tl_s, tl_r, v_s, v_r, w_s, w_r, vp_s, vp_r, a_s, a_r, g_s, g_r,
     l_s, l_r, m_s, m_r, x_s, x_r, r_s, r_r,
 ):
     pairs = n_img // 2
@@ -27,10 +27,8 @@
     p = me_i // 2
     c = lax.rem(me_i, 2)
     mate = 2 * p + 1 - c
-    et = img_ref.shape[0]
-    ei = txt_ref.shape[0]
-    rows = img_ref.shape[1]
-    cols = txt_ref.shape[1]
+    rows, et = img_ref.shape
+    cols, ei = txt_ref.shape
     part = rows // n_txt
 
     def img_of(k):
@@ -57,42 +55,79 @@
     def vis_rows(i):
         return pl.ds(pl.multiple_of(i * rows, rows), rows)
 
+    txt_rest[...] = jnp.zeros_like(txt_rest)
     barrier = pltpu.get_barrier_semaphore()
     for k in range(1, n_img):
         pl.semaphore_signal(barrier, inc=1, device_id=(img_of(k), me_t), device_id_type=MESH)
     for k in range(1, n_txt):
         pl.semaphore_signal(barrier, inc=1, device_id=(me_i, txt_of(k)), device_id_type=MESH)
+    text_own = txt_ref[...].T
+    text_high = text_own.astype(BF16)
+    txt_full[txt_rows(me_i), :] = text_high
+    img_full[img_rows(me_t), :] = img_ref[...].T.astype(BF16)
     pl.semaphore_wait(barrier, n_img + n_txt - 2)
+    txt_rest[txt_rows(me_i), :] = (text_own - text_high.astype(F32)).astype(BF16)
 
     mine_t = txt_full.at[txt_rows(me_i), :]
+    mine_x = img_full.at[img_rows(me_t), :]
+    mine_rest = txt_rest.at[txt_rows(me_i), :]
     text_z = [
-        remote(txt_ref, mine_t, t_s.at[k - 1], t_r.at[k - 1], 2 * pair_of(k) + c, me_t)
+        remote(mine_t, mine_t, t_s.at[k - 1], t_r.at[k - 1], 2 * pair_of(k) + c, me_t)
         for k in range(1, pairs)
     ]
-    text_mate = [remote(txt_ref, mine_t, tp_s.at[0], tp_r.at[0], mate, me_t)]
+    text_mate = [remote(mine_t, mine_t, tp_s.at[0], tp_r.at[0], mate, me_t)]
+    rest_mate = remote(mine_rest, mine_rest, tl_s.at[0], tl_r.at[0], mate, me_t)
     image_x = [
-        remote(img_ref, img_full.at[img_rows(me_t), :], i_s.at[k - 1], i_r.at[k - 1], me_i, txt_of(k))
+        remote(mine_x, mine_x, i_s.at[k - 1], i_r.at[k - 1], me_i, txt_of(k))
         for k in range(1, n_txt)
     ]
-    for copy in text_z + text_mate + image_x:
-        copy.start()
-    vis_ring = []
+    for copy in text_z + image_x + text_mate + [rest_mate]:
+        copy.start()
     vis_mate = []
 
+    def up_copy(step):
+        block = vis_full.at[vis_rows(2 * pair_of(-step) + c), :]
+        return remote(vis_ref if step == 0 else block, block, v_s.at[step], v_r.at[step], 2 * pair_of(1) + c, me_t)
+
+    def down_copy(step):
+        block = vis_full.at[vis_rows(2 * pair_of(step) + c), :]
+        return remote(vis_ref if step == 0 else block, block, w_s.at[step], w_r.at[step], 2 * pair_of(-1) + c, me_t)
+
+    def up_sends(step):
+        return jnp.logical_and(p - step >= 0, p < pairs - 1)
+
+    def down_sends(step):
+        return jnp.logical_and(p + step < pairs, p > 0)
+
+    def mate_copy(block, src, slot):
+        return remote(src, block, vp_s.at[slot], vp_r.at[slot], mate, me_t)
+
     def send_vis(step):
-        block = vis_rows(2 * pair_of(-step) + c)
-        src = vis_ref if step == 0 else vis_full.at[block, :]
+        if step == 0:
+            block = vis_full.at[vis_rows(me_i), :]
+            mate_copy(block, vis_ref, 0).start()
+        else:
+            @pl.when(p - step >= 0)
+            def _():
+                up_copy(step - 1).wait_recv()
+                block = vis_full.at[vis_rows(2 * pair_of(-step) + c), :]
+                mate_copy(block, block, step).start()
+
+            @pl.when(p + step < pairs)
+            def _():
+                down_copy(step - 1).wait_recv()
+                block = vis_full.at[vis_rows(2 * pair_of(step) + c), :]
+                mate_copy(block, block, pairs - 1 + step).start()
+
         if step < pairs - 1:
-            ring = remote(src, vis_full.at[block, :], v_s.at[step], v_r.at[step], 2 * pair_of(1) + c, me_t)
-            ring.start()
-            vis_ring.append(ring)
-        pair = remote(src, vis_full.at[block, :], vp_s.at[step], vp_r.at[step], mate, me_t)
-        pair.start()
-        vis_mate.append(pair)
-
-    send_vis(0)
-    txt_full[txt_rows(me_i), :] = txt_ref[...]
-    img_full[img_rows(me_t), :] = img_ref[...]
+            @pl.when(up_sends(step))
+            def _():
+                up_copy(step).start()
+
+            @pl.when(down_sends(step))
+            def _():
+                down_copy(step).start()
+
     vis_full[vis_rows(me_i), :] = vis_ref[...]
     for k in range(1, pairs):
         text_z[k - 1].wait_recv()
@@ -100,6 +135,7 @@
         copy = remote(block, block, tp_s.at[k], tp_r.at[k], mate, me_t)
         copy.start()
         text_mate.append(copy)
+    send_vis(0)
     for copy in image_x + text_mate:
         copy.wait_recv()
 
@@ -111,14 +147,18 @@
         image, text, (((0,), (0,)), ((), ())), preferred_element_type=F32
     ) + bias
     column = me_t * cols + lax.broadcasted_iota(jnp.int32, (rows, cols), 1)
-    sign = jnp.where(pos_ref[...] == column, 1.0, -1.0).astype(F32)
+    match = jnp.broadcast_to(pos_ref[...].astype(F32), (cols, rows)).T.astype(jnp.int32)
+    sign = jnp.where(match == column, 1.0, -1.0).astype(F32)
     slope = -sign / (1.0 + jnp.exp(sign * logits))
     high = slope.astype(BF16)
     rest = (slope - high.astype(F32)).astype(BF16)
 
     nt = (((1,), (1,)), ((), ()))
-    pimg[...] = lax.dot_general(high, text, nt, preferred_element_type=F32) + lax.dot_general(
-        rest, text, nt, preferred_element_type=F32
+    rest_mate.wait_recv()
+    pimg[...] = (
+        lax.dot_general(high, text, nt, preferred_element_type=F32)
+        + lax.dot_general(rest, text, nt, preferred_element_type=F32)
+        + lax.dot_general(high, txt_rest[...], nt, preferred_element_type=F32)
     )
 
     def part_rows(t):
@@ -141,12 +181,8 @@
     for copy in text_pair:
         copy.start()
 
-    def step_vis(step):
-        vis_ring[step - 1].wait_recv()
+    for step in range(1, pairs - 1):
         send_vis(step)
-
-    for step in range(1, pairs - 1):
-        step_vis(step)
 
     for copy in image_rs:
         copy.wait_recv()
@@ -170,6 +206,7 @@
         for k in range(1, n_txt)
     ]
     low_recv[me_i, me_t] = low_send[me_i]
+    send_vis(pairs - 1)
     for copy in low_z:
         copy.wait_recv()
     low_x = [
@@ -178,8 +215,6 @@
     ]
     for copy in low_x + grad_x:
         copy.start()
-
-    step_vis(pairs - 1)
 
     for q in range(pairs):
         text_pair[q].wait_recv()
@@ -192,15 +227,24 @@
     for copy in text_rs:
         copy.start()
 
-    for copy in low_x + vis_mate:
-        copy.wait_recv()
+    for copy in low_x:
+        copy.wait_recv()
+    mate_copy(vis_full.at[vis_rows(mate), :], vis_ref, 0).wait_recv()
+    for step in range(1, pairs):
+        @pl.when(p - step >= 0)
+        def _():
+            mate_copy(vis_full.at[vis_rows(mate), :], vis_ref, step).wait_recv()
+
+        @pl.when(p + step < pairs)
+        def _():
+            mate_copy(vis_full.at[vis_rows(mate), :], vis_ref, pairs - 1 + step).wait_recv()
     if part % 16:
         low_all = low_recv[...].astype(F32).reshape(n_img * rows, ei).astype(BF16)
     else:
         low_all = low_recv[...].reshape(n_img * rows, ei)
     gp_ref[...] = lax.dot_general(
         low_all, vis_full[...], (((0,), (0,)), ((), ())), preferred_element_type=F32
-    )
+    ).T
 
     for copy in grad_x:
         copy.wait_recv()
@@ -211,16 +255,33 @@
     total = txt_pair[p]
     for k in range(pairs - 1):
         total = total + rs_txt[k].astype(F32)
-    gt_ref[...] = scale * total
-    for copy in text_z + text_mate + image_x + vis_ring + vis_mate + image_rs + text_pair + low_z + low_x + grad_x + text_rs:
+    gt_ref[...] = (scale * total).T
+    for copy in text_z + text_mate + [rest_mate] + image_x + image_rs + text_pair + low_z + low_x + grad_x + text_rs:
         copy.wait_send()
+    mate_copy(vis_full.at[vis_rows(mate), :], vis_ref, 0).wait_send()
+    for step in range(pairs):
+        if step > 0:
+            @pl.when(p - step >= 0)
+            def _():
+                mate_copy(vis_full.at[vis_rows(mate), :], vis_ref, step).wait_send()
+
+            @pl.when(p + step < pairs)
+            def _():
+                mate_copy(vis_full.at[vis_rows(mate), :], vis_ref, pairs - 1 + step).wait_send()
+
+        if step < pairs - 1:
+            @pl.when(up_sends(step))
+            def _():
+                up_copy(step).wait_send()
+
+            @pl.when(down_sends(step))
+            def _():
+                down_copy(step).wait_send()
 
 
 def per_device(n_img, n_txt, image_emb, text_emb, vision_feat, positive, logit_scale, logit_bias):
-    image = image_emb.T.astype(BF16)
-    text = text_emb.T.astype(BF16)
-    et, rows = image.shape
-    ei, cols = text.shape
+    rows, et = image_emb.shape
+    cols, ei = text_emb.shape
     emb = et * n_txt
     vis = vision_feat.shape[1]
     part = rows // n_txt
@@ -232,13 +293,14 @@
         functools.partial(kernel, n_img, n_txt),
         out_shape=(
             jax.ShapeDtypeStruct((n_txt, part, et), F32),
-            jax.ShapeDtypeStruct((ei, cols), F32),
-            jax.ShapeDtypeStruct((ei, vis), F32),
+            jax.ShapeDtypeStruct((cols, ei), F32),
+            jax.ShapeDtypeStruct((vis, ei), F32),
         ),
         in_specs=[smem, smem, vmem, vmem, vmem, vmem],
         out_specs=(vmem, vmem, vmem),
         scratch_shapes=[
             pltpu.VMEM((emb, rows), BF16),
+            pltpu.VMEM((emb, cols), BF16),
             pltpu.VMEM((emb, cols), BF16),
             pltpu.VMEM((n_img * rows, vis), BF16),
             pltpu.VMEM((rows, emb), F32),
@@ -252,8 +314,8 @@
             pltpu.VMEM((pairs, ei, cols), BF16),
             pltpu.VMEM((pairs - 1, ei, cols), BF16),
             dma(n_txt - 1), dma(n_txt - 1),
-            dma(pairs - 1), dma(pairs - 1), dma(pairs), dma(pairs),
-            dma(pairs - 1), dma(pairs - 1), dma(pairs), dma(pairs),
+            dma(pairs - 1), dma(pairs - 1), dma(pairs), dma(pairs), dma(1), dma(1),
+            dma(pairs - 1), dma(pairs - 1), dma(pairs - 1), dma(pairs - 1), dma(2 * pairs - 1), dma(2 * pairs - 1),
             dma(n_txt - 1), dma(n_txt - 1), dma(n_txt - 1), dma(n_txt - 1),
             dma(n_img - 1), dma(n_img - 1), dma(n_txt - 1), dma(n_txt - 1),
             dma(pairs), dma(pairs), dma(pairs - 1), dma(pairs - 1),
@@ -261,8 +323,8 @@
         compiler_params=pltpu.CompilerParams(
             collective_id=0, has_side_effects=True, vmem_limit_bytes=60 * 1024 * 1024
         ),
-    )(logit_scale, logit_bias, positive.reshape(rows, 1), image, text, vision_feat)
-    return gi.reshape(rows, et), gt.T, gp.T
+    )(logit_scale, logit_bias, positive.reshape(1, rows), image_emb, text_emb, vision_feat)
+    return gi.reshape(rows, et), gt, gp
 
 
 def solution(mesh):

time: 76.7 us -> 67.3 us (0.88)
  Pallas kernels: 66.2 us -> 58.3 us
    pallas_call x1, Pallas kernels: 66.2 us -> 58.3 us  [per_device(): pl.pallas_call(functools.partial(kernel, n_img, n_txt), out_shape=(jax.Sh...]
    reshape x1 -> x0, local copies, waits for them, and re-layouts: 1.39 us -> none  [per_device(): positive.reshape(rows, 1)]
    unnamed x8 -> x6, local copies, waits for them, and re-layouts: 6.22 us -> 6.87 us
where the time goes in v2:
time: 67.3 us; the launch traced here: 67.1 us
  Pallas kernels  58.3 us (87%)
  local copies, waits for them, and re-layouts  6.87 us (10%)
  between operations  1.94 us (3%)
    pallas_call x1, Pallas kernels, per_device(): pl.pallas_call(functools.partial(kernel, n_img, n_txt), out_shape=(jax.Sh...  58.3 us
    unnamed x6, local copies, waits for them, and re-layouts  6.87 us

profile of v2, /device:TPU:0, one launch (start us, length us, event | category | flops | bytes accessed | tf_op | source)
XLA Modules:
  0.0 67.1 jit_solution(3953579381866891464)
XLA Ops:
  1.9 1.8 %copy.9.txt_ref = f32[256,192]{1,0:T(8,128)} copy(f32[256,192]{0,1:T(8,128)} %param.7) | data formatting | bytes 393216 | tf_op args[1]
  3.7 58.3 %shard_map.85 = (f32[4,32,384]{2,1,0:T(8,128)}, f32[256,192]{1,0:T(8,128)}, f32[1280,192]{1,0:T(8,128)}) custom-call(f32[1]{0:T(128)S(6)} %copy.13.scale_ref, f32[1]{0:T(128)S(6)} %copy.14.bias_ref, s32[1,128]{1,0:T(1,128)} %bitcast.3, f32[128,384]{1,0:T(8,128)} %img_ref.1, f32[256,192]{1,0:T(8,128)} %copy.9.txt_ref, bf16[128,1280]{1,0:T(8,128)(2,1)} %vis_ref.1), custom_call_target="tpu_custom_call" | custom-call | tf_op jit(solution)/shard_map/pallas_call | solution.py:292
  61.9 0.0 copy-start
  62.0 1.8 %copy.10 = f32[256,192]{0,1:T(8,128)} copy(f32[256,192]{1,0:T(8,128)} %get-tuple-element.10) | data formatting | bytes 393216
  63.7 2.6 %copy.11 = f32[1280,192]{0,1:T(8,128)} copy(f32[1280,192]{1,0:T(8,128)} %get-tuple-element.11) | data formatting | bytes 1966080
  66.4 0.0 copy-done
  66.4 0.7 %copy.15 = f32[128,384]{1,0:T(8,128)} copy(f32[128,384]{1,0:T(8,128)S(1)} %bitcast.2) | data formatting | bytes 393216
Async XLA Ops:
  61.9 4.4 %copy-start = (f32[4,32,384]{2,1,0:T(8,128)S(1)}, f32[4,32,384]{2,1,0:T(8,128)}, u32[]{:S(2)}) copy-start(f32[4,32,384]{2,1,0:T(8,128)} %get-tuple-element.6) | copy-start | bytes 589828

commit v3 on v2

--- a/solution.py
+++ b/solution.py
@@ -8,6 +8,7 @@
 from jax.sharding import PartitionSpec as P
 
 MESH = pl.DeviceIdType.MESH
+PIECES = 2
 F32 = jnp.float32
 BF16 = jnp.bfloat16
 
@@ -28,8 +29,9 @@
     c = lax.rem(me_i, 2)
     mate = 2 * p + 1 - c
     rows, et = img_ref.shape
-    cols, ei = txt_ref.shape
+    ei, cols = txt_ref.shape
     part = rows // n_txt
+    piece = rows // PIECES
 
     def img_of(k):
         return lax.rem(me_i + k, n_img)
@@ -52,8 +54,8 @@
     def img_rows(t):
         return pl.ds(pl.multiple_of(t * et, et), et)
 
-    def vis_rows(i):
-        return pl.ds(pl.multiple_of(i * rows, rows), rows)
+    def vis_rows(i, h):
+        return pl.ds(pl.multiple_of(i * rows + h * piece, piece), piece)
 
     txt_rest[...] = jnp.zeros_like(txt_rest)
     barrier = pltpu.get_barrier_semaphore()
@@ -61,7 +63,7 @@
         pl.semaphore_signal(barrier, inc=1, device_id=(img_of(k), me_t), device_id_type=MESH)
     for k in range(1, n_txt):
         pl.semaphore_signal(barrier, inc=1, device_id=(me_i, txt_of(k)), device_id_type=MESH)
-    text_own = txt_ref[...].T
+    text_own = txt_ref[...]
     text_high = text_own.astype(BF16)
     txt_full[txt_rows(me_i), :] = text_high
     img_full[img_rows(me_t), :] = img_ref[...].T.astype(BF16)
@@ -85,13 +87,18 @@
         copy.start()
     vis_mate = []
 
-    def up_copy(step):
-        block = vis_full.at[vis_rows(2 * pair_of(-step) + c), :]
-        return remote(vis_ref if step == 0 else block, block, v_s.at[step], v_r.at[step], 2 * pair_of(1) + c, me_t)
-
-    def down_copy(step):
-        block = vis_full.at[vis_rows(2 * pair_of(step) + c), :]
-        return remote(vis_ref if step == 0 else block, block, w_s.at[step], w_r.at[step], 2 * pair_of(-1) + c, me_t)
+    def up_copy(step, h):
+        block = vis_full.at[vis_rows(2 * pair_of(-step) + c, h), :]
+        n = step * PIECES + h
+        return remote(vis_own(h) if step == 0 else block, block, v_s.at[n], v_r.at[n], 2 * pair_of(1) + c, me_t)
+
+    def down_copy(step, h):
+        block = vis_full.at[vis_rows(2 * pair_of(step) + c, h), :]
+        n = step * PIECES + h
+        return remote(vis_own(h) if step == 0 else block, block, w_s.at[n], w_r.at[n], 2 * pair_of(-1) + c, me_t)
+
+    def vis_own(h):
+        return vis_ref.at[pl.ds(h * piece, piece), :]
 
     def up_sends(step):
         return jnp.logical_and(p - step >= 0, p < pairs - 1)
@@ -99,43 +106,50 @@
     def down_sends(step):
         return jnp.logical_and(p + step < pairs, p > 0)
 
-    def mate_copy(block, src, slot):
-        return remote(src, block, vp_s.at[slot], vp_r.at[slot], mate, me_t)
-
-    def send_vis(step):
+    def mate_copy(offset, h):
+        block = vis_full.at[vis_rows(2 * pair_of(-offset) + c, h), :]
+        n = (offset if offset >= 0 else pairs - 1 - offset) * PIECES + h
+        return remote(vis_own(h) if offset == 0 else block, block, vp_s.at[n], vp_r.at[n], mate, me_t)
+
+    def send_vis(step, h):
         if step == 0:
-            block = vis_full.at[vis_rows(me_i), :]
-            mate_copy(block, vis_ref, 0).start()
+            mate_copy(0, h).start()
         else:
             @pl.when(p - step >= 0)
             def _():
-                up_copy(step - 1).wait_recv()
-                block = vis_full.at[vis_rows(2 * pair_of(-step) + c), :]
-                mate_copy(block, block, step).start()
+                up_copy(step - 1, h).wait_recv()
 
             @pl.when(p + step < pairs)
             def _():
-                down_copy(step - 1).wait_recv()
-                block = vis_full.at[vis_rows(2 * pair_of(step) + c), :]
-                mate_copy(block, block, pairs - 1 + step).start()
+                down_copy(step - 1, h).wait_recv()
 
         if step < pairs - 1:
             @pl.when(up_sends(step))
             def _():
-                up_copy(step).start()
+                up_copy(step, h).start()
 
             @pl.when(down_sends(step))
             def _():
-                down_copy(step).start()
-
-    vis_full[vis_rows(me_i), :] = vis_ref[...]
+                down_copy(step, h).start()
+
+        if step > 0:
+            @pl.when(p - step >= 0)
+            def _():
+                mate_copy(step, h).start()
+
+            @pl.when(p + step < pairs)
+            def _():
+                mate_copy(-step, h).start()
+
+    for h in range(PIECES):
+        send_vis(0, h)
+    vis_full[pl.ds(pl.multiple_of(me_i * rows, rows), rows), :] = vis_ref[...]
     for k in range(1, pairs):
         text_z[k - 1].wait_recv()
         block = txt_full.at[txt_rows(2 * pair_of(-k) + c), :]
         copy = remote(block, block, tp_s.at[k], tp_r.at[k], mate, me_t)
         copy.start()
         text_mate.append(copy)
-    send_vis(0)
     for copy in image_x + text_mate:
         copy.wait_recv()
 
@@ -182,7 +196,8 @@
         copy.start()
 
     for step in range(1, pairs - 1):
-        send_vis(step)
+        for h in range(PIECES):
+            send_vis(step, h)
 
     for copy in image_rs:
         copy.wait_recv()
@@ -206,7 +221,6 @@
         for k in range(1, n_txt)
     ]
     low_recv[me_i, me_t] = low_send[me_i]
-    send_vis(pairs - 1)
     for copy in low_z:
         copy.wait_recv()
     low_x = [
@@ -215,6 +229,9 @@
     ]
     for copy in low_x + grad_x:
         copy.start()
+
+    for h in range(PIECES):
+        send_vis(pairs - 1, h)
 
     for q in range(pairs):
         text_pair[q].wait_recv()
@@ -229,22 +246,23 @@
 
     for copy in low_x:
         copy.wait_recv()
-    mate_copy(vis_full.at[vis_rows(mate), :], vis_ref, 0).wait_recv()
-    for step in range(1, pairs):
-        @pl.when(p - step >= 0)
-        def _():
-            mate_copy(vis_full.at[vis_rows(mate), :], vis_ref, step).wait_recv()
-
-        @pl.when(p + step < pairs)
-        def _():
-            mate_copy(vis_full.at[vis_rows(mate), :], vis_ref, pairs - 1 + step).wait_recv()
+    for h in range(PIECES):
+        mate_copy(0, h).wait_recv()
+        for step in range(1, pairs):
+            @pl.when(p - step >= 0)
+            def _():
+                mate_copy(step, h).wait_recv()
+
+            @pl.when(p + step < pairs)
+            def _():
+                mate_copy(-step, h).wait_recv()
     if part % 16:
         low_all = low_recv[...].astype(F32).reshape(n_img * rows, ei).astype(BF16)
     else:
         low_all = low_recv[...].reshape(n_img * rows, ei)
     gp_ref[...] = lax.dot_general(
         low_all, vis_full[...], (((0,), (0,)), ((), ())), preferred_element_type=F32
-    ).T
+    )
 
     for copy in grad_x:
         copy.wait_recv()
@@ -255,28 +273,29 @@
     total = txt_pair[p]
     for k in range(pairs - 1):
         total = total + rs_txt[k].astype(F32)
-    gt_ref[...] = (scale * total).T
+    gt_ref[...] = scale * total
     for copy in text_z + text_mate + [rest_mate] + image_x + image_rs + text_pair + low_z + low_x + grad_x + text_rs:
         copy.wait_send()
-    mate_copy(vis_full.at[vis_rows(mate), :], vis_ref, 0).wait_send()
-    for step in range(pairs):
-        if step > 0:
-            @pl.when(p - step >= 0)
-            def _():
-                mate_copy(vis_full.at[vis_rows(mate), :], vis_ref, step).wait_send()
-
-            @pl.when(p + step < pairs)
-            def _():
-                mate_copy(vis_full.at[vis_rows(mate), :], vis_ref, pairs - 1 + step).wait_send()
-
-        if step < pairs - 1:
-            @pl.when(up_sends(step))
-            def _():
-                up_copy(step).wait_send()
-
-            @pl.when(down_sends(step))
-            def _():
-                down_copy(step).wait_send()
+    for h in range(PIECES):
+        mate_copy(0, h).wait_send()
+        for step in range(pairs):
+            if step > 0:
+                @pl.when(p - step >= 0)
+                def _():
+                    mate_copy(step, h).wait_send()
+
+                @pl.when(p + step < pairs)
+                def _():
+                    mate_copy(-step, h).wait_send()
+
+            if step < pairs - 1:
+                @pl.when(up_sends(step))
+                def _():
+                    up_copy(step, h).wait_send()
+
+                @pl.when(down_sends(step))
+                def _():
+                    down_copy(step, h).wait_send()
 
 
 def per_device(n_img, n_txt, image_emb, text_emb, vision_feat, positive, logit_scale, logit_bias):
@@ -293,8 +312,8 @@
         functools.partial(kernel, n_img, n_txt),
         out_shape=(
             jax.ShapeDtypeStruct((n_txt, part, et), F32),
-            jax.ShapeDtypeStruct((cols, ei), F32),
-            jax.ShapeDtypeStruct((vis, ei), F32),
+            jax.ShapeDtypeStruct((ei, cols), F32),
+            jax.ShapeDtypeStruct((ei, vis), F32),
         ),
         in_specs=[smem, smem, vmem, vmem, vmem, vmem],
         out_specs=(vmem, vmem, vmem),
@@ -315,7 +334,7 @@
             pltpu.VMEM((pairs - 1, ei, cols), BF16),
             dma(n_txt - 1), dma(n_txt - 1),
             dma(pairs - 1), dma(pairs - 1), dma(pairs), dma(pairs), dma(1), dma(1),
-            dma(pairs - 1), dma(pairs - 1), dma(pairs - 1), dma(pairs - 1), dma(2 * pairs - 1), dma(2 * pairs - 1),
+            *[dma(PIECES * (pairs - 1))] * 4, *[dma(PIECES * (2 * pairs - 1))] * 2,
             dma(n_txt - 1), dma(n_txt - 1), dma(n_txt - 1), dma(n_txt - 1),
             dma(n_img - 1), dma(n_img - 1), dma(n_txt - 1), dma(n_txt - 1),
             dma(pairs), dma(pairs), dma(pairs - 1), dma(pairs - 1),
@@ -323,8 +342,8 @@
         compiler_params=pltpu.CompilerParams(
             collective_id=0, has_side_effects=True, vmem_limit_bytes=60 * 1024 * 1024
         ),
-    )(logit_scale, logit_bias, positive.reshape(1, rows), image_emb, text_emb, vision_feat)
-    return gi.reshape(rows, et), gt, gp
+    )(logit_scale, logit_bias, positive.reshape(1, rows), image_emb, text_emb.T, vision_feat)
+    return gi.reshape(rows, et), gt.T, gp.T
 
 
 def solution(mesh):

time: 67.3 us -> 60.9 us (0.905)
  Pallas kernels: 58.3 us -> 54.2 us
  local copies, waits for them, and re-layouts: 6.87 us -> 4.54 us
    pallas_call x1, Pallas kernels: 58.3 us -> 54.2 us  [per_device(): pl.pallas_call(functools.partial(kernel, n_img, n_txt), out_shape=(jax.Sh...]
    unnamed x6 -> x5, local copies, waits for them, and re-layouts: 6.87 us -> 4.54 us
where the time goes in v3:
time: 60.9 us; the launch traced here: 60.7 us
  Pallas kernels  54.2 us (89%)
  local copies, waits for them, and re-layouts  4.54 us (7%)
  between operations  1.94 us (3%)
    pallas_call x1, Pallas kernels, per_device(): pl.pallas_call(functools.partial(kernel, n_img, n_txt), out_shape=(jax.Sh...  54.2 us
    unnamed x5, local copies, waits for them, and re-layouts  4.54 us

profile of v3, /device:TPU:0, one launch (start us, length us, event | category | flops | bytes accessed | tf_op | source)
XLA Modules:
  0.0 60.7 jit_solution(3763298831145133626)
XLA Ops:
  1.9 54.2 %shard_map.85 = (f32[4,32,384]{2,1,0:T(8,128)}, f32[192,256]{1,0:T(8,128)}, f32[192,1280]{1,0:T(8,128)}) custom-call(f32[1]{0:T(128)S(6)} %copy.12.scale_ref, f32[1]{0:T(128)S(6)} %copy.13.bias_ref, s32[1,128]{1,0:T(1,128)} %bitcast.9, f32[128,384]{1,0:T(8,128)} %img_ref.1, f32[192,256]{1,0:T(8,128)} %bitcast.8, bf16[128,1280]{1,0:T(8,128)(2,1)} %vis_ref.1), custom_call_target="tpu_custom_call" | custom-call | tf_op jit(solution)/shard_map/pallas_call | solution.py:311
  56.1 0.0 copy-start
  56.1 1.7 %copy.14 = f32[128,384]{1,0:T(8,128)} copy(f32[128,384]{1,0:T(8,128)} %bitcast.7) | data formatting | bytes 393216
  57.8 0.0 copy-done
  57.8 0.7 %copy.15 = f32[256,192]{0,1:T(8,128)} copy(f32[256,192]{0,1:T(8,128)S(1)} %bitcast.6) | data formatting | bytes 393216
  58.5 2.2 %copy.16 = f32[1280,192]{0,1:T(8,128)} copy(f32[1280,192]{0,1:T(8,128)} %bitcast.5) | data formatting | bytes 1966080
Async XLA Ops:
  56.1 1.7 %copy-start = (f32[192,256]{1,0:T(8,128)S(1)}, f32[192,256]{1,0:T(8,128)}, u32[]{:S(2)}) copy-start(f32[192,256]{1,0:T(8,128)} %get-tuple-element.7) | copy-start | bytes 589828

commit v4 on v3

--- a/solution.py
+++ b/solution.py
@@ -8,7 +8,7 @@
 from jax.sharding import PartitionSpec as P
 
 MESH = pl.DeviceIdType.MESH
-PIECES = 2
+PIECES = 4
 F32 = jnp.float32
 BF16 = jnp.bfloat16
 
@@ -185,6 +185,9 @@
     for copy in image_rs:
         copy.start()
 
+    for step in range(1, pairs - 1):
+        for h in range(PIECES):
+            send_vis(step, h)
     ptxt[...] = jnp.dot(image, high, preferred_element_type=F32) + jnp.dot(
         image, rest, preferred_element_type=F32
     )
@@ -195,9 +198,6 @@
     for copy in text_pair:
         copy.start()
 
-    for step in range(1, pairs - 1):
-        for h in range(PIECES):
-            send_vis(step, h)
 
     for copy in image_rs:
         copy.wait_recv()

time: 60.9 us -> 59.2 us (0.972)
  Pallas kernels: 54.2 us -> 52.5 us
    pallas_call x1, Pallas kernels: 54.2 us -> 52.5 us  [per_device(): pl.pallas_call(functools.partial(kernel, n_img, n_txt), out_shape=(jax.Sh...]
where the time goes in v4:
time: 59.2 us; the launch traced here: 59 us
  Pallas kernels  52.5 us (89%)
  local copies, waits for them, and re-layouts  4.54 us (8%)
  between operations  1.94 us (3%)
    pallas_call x1, Pallas kernels, per_device(): pl.pallas_call(functools.partial(kernel, n_img, n_txt), out_shape=(jax.Sh...  52.5 us
    unnamed x5, local copies, waits for them, and re-layouts  4.54 us

profile of v4, /device:TPU:0, one launch (start us, length us, event | category | flops | bytes accessed | tf_op | source)
XLA Modules:
  0.0 59.0 jit_solution(13366342971876217466)
XLA Ops:
  1.9 52.5 %shard_map.85 = (f32[4,32,384]{2,1,0:T(8,128)}, f32[192,256]{1,0:T(8,128)}, f32[192,1280]{1,0:T(8,128)}) custom-call(f32[1]{0:T(128)S(6)} %copy.12.scale_ref, f32[1]{0:T(128)S(6)} %copy.13.bias_ref, s32[1,128]{1,0:T(1,128)} %bitcast.9, f32[128,384]{1,0:T(8,128)} %img_ref.1, f32[192,256]{1,0:T(8,128)} %bitcast.8, bf16[128,1280]{1,0:T(8,128)(2,1)} %vis_ref.1), custom_call_target="tpu_custom_call" | custom-call | tf_op jit(solution)/shard_map/pallas_call | solution.py:311
  54.4 0.0 copy-start
  54.5 1.7 %copy.14 = f32[128,384]{1,0:T(8,128)} copy(f32[128,384]{1,0:T(8,128)} %bitcast.7) | data formatting | bytes 393216
  56.1 0.0 copy-done
  56.1 0.7 %copy.15 = f32[256,192]{0,1:T(8,128)} copy(f32[256,192]{0,1:T(8,128)S(1)} %bitcast.6) | data formatting | bytes 393216
  56.8 2.2 %copy.16 = f32[1280,192]{0,1:T(8,128)} copy(f32[1280,192]{0,1:T(8,128)} %bitcast.5) | data formatting | bytes 1966080
Async XLA Ops:
  54.4 1.7 %copy-start = (f32[192,256]{1,0:T(8,128)S(1)}, f32[192,256]{1,0:T(8,128)}, u32[]{:S(2)}) copy-start(f32[192,256]{1,0:T(8,128)} %get-tuple-element.7) | copy-start | bytes 589828
